TPU v7x, 32 devices: a whole 2x2x4 slice. The times are simulated.
32 devices in a mesh: mesh: 8 (over z, core), src: 4 (over y, x).
Axes of the slice: x: 2, y: 2, z: 4, core: 2. Of those that a mesh axis runs over, the one named last changes fastest.
Arguments:
- solution: float32 [512, 24576], P('src', 'mesh'), may hold values from -6 to 6
- conduct: float32 [24576], P('mesh'), may hold values from 0.5 to 2
- source_edge: int32 [512], P('src'), may hold values from 0 to 24575
- source_amp: float32 [512], P('src'), may hold values from -8 to 8
- interior: int32 [8192], P('mesh'), may hold values 0 or 1
- edge_dir: float32 [3, 24576], P(None, 'mesh'), may hold values from -4 to 4
- tail_node: int32 [24576], P('mesh'), may hold values from 0 to 127, as said below
- head_node: int32 [24576], P('mesh'), may hold values from 0 to 383, as said below
- block_inv: float32 [256, 128, 128], P(('mesh', 'src')), may hold values from -1 to 1
- block_op: float32 [256, 128, 128], P(('mesh', 'src')), may hold values from -1 to 4
Outputs:
- correction: float32 [512, 24576], P('src', 'mesh')
Inputs may be any that keep to these rules, and one draw needn't show every extreme that they name: `tail_node`: every value occurs. An edge of block k has head_node of (2 - k) * 128 or more; head_node never equals 256 + tail_node.
All inputs are finite; a program needn't handle non-finite values. No bound on the sum of `interior` on one device may be relied on, other than what follows from the above.
Results may differ from a plain program's by a relative error of at most 0.0034.
Values may be sent and summed in bfloat16 or wider, within the bound.
No kernel may reach another device: no remote copies, remote signals or barrier semaphores. Data moves between devices by JAX's collectives and lax.ppermute only.
A program may use at most 64 MiB of HBM per device.

v0:
```python
import jax
import jax.numpy as jnp
from jax import lax
from jax.sharding import PartitionSpec as P

BLOCK_NODES = 128
TILES_BLOCK = 3
HIGHEST_PREC = lax.Precision.HIGHEST


def shifted(x, axis, by):
    peers = lax.axis_size(axis)
    pairs = [(i, i + by) for i in range(peers) if 0 <= i + by < peers]
    return lax.ppermute(x, axis, pairs)


def spread_heads(head_part, bnodes):
    row_count = head_part.shape[0]
    running = jnp.zeros((row_count + 2,) + head_part.shape[1:3] + (bnodes,), jnp.float32)
    for offset in range(3):
        slab_part = head_part[..., offset * bnodes : (offset + 1) * bnodes]
        running = running + jnp.pad(slab_part, ((offset, 2 - offset), (0, 0), (0, 0), (0, 0)))
    return running


def endpoint_coefs(directions, nblocks, edge_span):
    half_dir = 0.5 * directions.reshape(3, nblocks, edge_span)
    unit_row = jnp.ones((1, nblocks, edge_span), jnp.float32)
    return (jnp.concatenate([-unit_row, half_dir], 0), jnp.concatenate([unit_row, half_dir], 0))


def block_sweep(nodal_rhs, inverse, operator):
    rhs_full = nodal_rhs.astype(jnp.float32)
    first_pass = jnp.einsum("ism,inm->isn", rhs_full, inverse, precision=HIGHEST_PREC)
    defect = rhs_full - jnp.einsum("ism,inm->isn", first_pass, operator, precision=HIGHEST_PREC)
    solved = first_pass + jnp.einsum("ism,inm->isn", defect, inverse, precision=HIGHEST_PREC)
    return solved.astype(jnp.bfloat16)


def shards(
    solution,
    conduct,
    source_edge,
    source_amp,
    interior,
    edge_dir,
    tail_node,
    head_node,
    block_inv,
    block_op,
):
    src_dev, edge_dev = solution.shape
    bnodes = BLOCK_NODES
    edge_span = TILES_BLOCK * bnodes
    nblocks = edge_dev // edge_span
    first_edge = lax.axis_index("mesh") * edge_dev
    edge_ids = first_edge + lax.iota(jnp.int32, edge_dev)
    source_hit = source_edge[:, None] == edge_ids[None, :]
    residual = jnp.where(source_hit, source_amp[:, None], 0.0) - conduct[None, :] * solution
    resid_blocks = residual.reshape(src_dev, nblocks, edge_span)
    coef_tail, coef_head = endpoint_coefs(edge_dir, nblocks, edge_span)
    tail_match = tail_node.reshape(nblocks, edge_span)[:, :, None] == lax.iota(jnp.int32, bnodes)
    head_match = head_node.reshape(nblocks, edge_span)[:, :, None] == lax.iota(
        jnp.int32, 3 * bnodes
    )
    tail_hot = tail_match.astype(jnp.float32)
    head_hot = head_match.astype(jnp.float32)
    tail_part = jnp.einsum(
        "fske,ken->kfsn", coef_tail[:, None] * resid_blocks[None], tail_hot, precision=HIGHEST_PREC
    )
    head_part = jnp.einsum(
        "fske,ken->kfsn", coef_head[:, None] * resid_blocks[None], head_hot, precision=HIGHEST_PREC
    )
    padded = spread_heads(head_part, bnodes)
    nodal_sum = padded[2:] + tail_part
    rim_sum = shifted(padded[:2], "mesh", -1)
    nodal_sum = jnp.concatenate([nodal_sum[: nblocks - 2], nodal_sum[nblocks - 2 :] + rim_sum], 0)
    keep_mask = interior.reshape(nblocks, 1, 1, bnodes)
    restricted = (nodal_sum * keep_mask.astype(jnp.float32)).astype(jnp.bfloat16)
    restricted = restricted.reshape(nblocks * 4, src_dev, bnodes)
    grouped = lax.all_to_all(restricted, "src", split_axis=0, concat_axis=1, tiled=True)
    solved = block_sweep(grouped, block_inv, block_op)
    nodal = lax.all_to_all(solved, "src", split_axis=1, concat_axis=0, tiled=True)
    nodal = nodal.reshape(nblocks, 4, src_dev, bnodes) * keep_mask.astype(jnp.bfloat16)
    earlier = shifted(nodal[nblocks - 2 :], "mesh", 1)
    padded_corr = jnp.concatenate([earlier, nodal], 0)
    tail_low = tail_match.astype(jnp.bfloat16)
    head_low = head_match.astype(jnp.bfloat16).reshape(nblocks, edge_span, 3, bnodes)
    tail_vals = jnp.einsum(
        "kfsn,ken->fske", padded_corr[2:], tail_low, preferred_element_type=jnp.float32
    )
    windows = jnp.stack([padded_corr[offset : offset + nblocks] for offset in range(3)], 0)
    head_vals = jnp.einsum(
        "jkfsn,kejn->fske", windows, head_low, preferred_element_type=jnp.float32
    )
    summed = jnp.sum(coef_tail[:, None] * tail_vals + coef_head[:, None] * head_vals, axis=0)
    return summed.reshape(src_dev, edge_dev)


def solution(mesh):
    placed = (
        P("src", "mesh"),
        P("mesh"),
        P("src"),
        P("src"),
        P("mesh"),
        P(None, "mesh"),
        P("mesh"),
        P("mesh"),
        P(("mesh", "src"), None, None),
        P(("mesh", "src"), None, None),
    )
    return jax.shard_map(
        shards, mesh=mesh, in_specs=placed, out_specs=P("src", "mesh"), check_vma=False
    )
```

profile of v0, /device:TPU:1, one launch (start us, length us, event | category | flops | bytes accessed | tf_op | source)
XLA Modules:
  0.0 91.9 jit_solution(16786728489836537764)
XLA Ops:
  0.0 0.9 broadcast_multiply_fusion.2
  0.9 2.9 %multiply_subtract_fusion = f32[128,3072]{1,0:T(8,128)} fusion(f32[128,3072]{1,0:T(8,128)} %param.10, f32[3072]{0:T(1024)} %param.11, f32[128]{0:T(128)} %param.13, s32[3072]{0:T(1024)S(1)} %iota_add_fusion, s32[128]{0:T(128)} %param.12), kind=kLoop, calls=%fused_computation.34 | loop fusion | flops 1572864 | bytes 3171328 | tf_op jit(solution)/shard_map/sub | solution.py:59
  3.8 1.9 %copy.36 = f32[128,3072]{0,1:T(8,128)S(1)} copy(f32[128,3072]{1,0:T(8,128)} %multiply_subtract_fusion) | data formatting | bytes 3145728 | tf_op jit(solution)/shard_map/mul | solution.py:72
  5.7 11.7 %fusion.4 = f32[8,4,128,384]{3,2,1,0:T(8,128)S(1)} fusion(f32[128,8,384]{0,2,1:T(8,128)S(1)} %bitcast.66, f32[4,8,384]{2,0,1:T(4,128)S(1)} %get-tuple-element.11, s32[8,384]{1,0:T(8,128)S(1)} %eq.63), kind=kOutput, calls=%fused_computation.6 | convolution fusion | flops 7250509824 | bytes 7925760 | tf_op jit(solution)/shard_map/fske,ken->kfsn/dot_general | solution.py:71
  17.4 0.9 fusion.45
  18.3 1.9 %collective-permute-start = (f32[2,4,128,128]{3,2,1,0:T(8,128)S(1)}, f32[2,4,128,128]{3,2,1,0:T(8,128)S(1)}, u32[]{:S(2)}, u32[]{:S(2)}) collective-permute-start(f32[2,4,128,128]{3,2,1,0:T(8,128)S(1)} %pad_add_fusion.1), channel_id=1, source_target_pairs={{4,0},{8,4},{12,8},{16,12},{20,16},{24,20},{28,24},{5,1},{9,5},{13... | collective-permute-start | bytes 1572872 | tf_op jit(solution)/shard_map/ppermute | solution.py:14
  20.3 2.0 %pad_add_fusion = f32[10,4,128,128]{3,2,1,0:T(8,128)} fusion(f32[8,4,128,128]{3,2,1,0:T(8,128)S(1)} %get-tuple-element.6, f32[8,4,128,128]{3,2,1,0:T(8,128)S(1)} %get-tuple-element.7, f32[8,4,128,128]{3,2,1,0:T(8,128)S(1)} %get-tuple-element.5), kind=kLoop, calls=%fused_computation.22 | loop fusion | flops 1310720 | bytes 8912896 | tf_op jit(solution)/shard_map/add | solution.py:22
  22.3 9.9 %slice_add_fusion = f32[8,4,128,128]{3,2,1,0:T(8,128)S(1)} fusion(f32[10,4,128,128]{3,2,1,0:T(8,128)} %pad_add_fusion, f32[128,8,384]{0,2,1:T(8,128)S(1)} %bitcast.67, f32[4,8,384]{2,0,1:T(4,128)S(1)} %get-tuple-element.10, s32[8,384]{1,0:T(8,128)S(1)} %eq.56), kind=kOutput, calls=%fused_computation.26 | convolution fusion | flops 2418409472 | bytes 5828608 | tf_op jit(solution)/shard_map/fske,ken->kfsn/dot_general | solution.py:68
  32.3 0.6 copy-done.4
  33.0 0.2 pad_maximum_fusion
  33.2 0.3 fusion.23
  33.5 19.0 %all_to_all.33 = bf16[32,128,128]{2,1,0:T(8,128)(2,1)S(1)} all-to-all(bf16[32,128,128]{2,1,0:T(8,128)(2,1)S(1)} %fusion.23), channel_id=1, replica_groups=mesh['mesh'=8,'src'=4] {'src'}, dimensions={0} | all-to-all | bytes 2097152 | tf_op jit(solution)/shard_map/all_to_all | solution.py:81
  52.5 1.0 %fusion.47 = f32[8,512,128]{2,1,0:T(8,128)S(1)} fusion(bf16[8,512,128]{2,1,0:T(8,128)(2,1)S(1)} %bitcast.70, f32[8,128,128]{2,1,0:T(8,128)S(1)} %copy-done), kind=kOutput, calls=%fused_computation.58 | convolution fusion | flops 805306368 | bytes 3670016 | tf_op jit(solution)/shard_map/ism,inm->isn/dot_general | solution.py:34
  53.6 2.0 %fusion.48 = f32[8,512,128]{2,1,0:T(8,128)S(1)} fusion(f32[8,512,128]{2,1,0:T(8,128)S(1)} %fusion.47, f32[8,128,128]{2,1,0:T(8,128)S(1)} %copy-done.1), kind=kOutput, calls=%fused_computation.59 | convolution fusion | flops 805306368 | bytes 4718592 | tf_op jit(solution)/shard_map/ism,inm->isn/dot_general | solution.py:35
  55.5 2.2 %add_convert_fusion = bf16[8,512,128]{2,1,0:T(8,128)(2,1)S(1)} fusion(f32[8,512,128]{2,1,0:T(8,128)S(1)} %fusion.47, f32[8,128,128]{2,1,0:T(8,128)S(1)} %copy-done, f32[8,512,128]{2,1,0:T(8,128)S(1)} %fusion.48, bf16[8,512,128]{2,1,0:T(8,128)(2,1)S(1)} %bitcast.71), kind=kOutput, calls=%fused_computation.30 | convolution fusion | flops 807403520 | bytes 6815744 | tf_op jit(solution)/shard_map/ism,inm->isn/dot_general | solution.py:36
  57.8 1.6 %copy.26 = bf16[8,512,128]{2,0,1:T(8,128)(2,1)} copy(bf16[8,512,128]{2,1,0:T(8,128)(2,1)S(1)} %add_convert_fusion) | data formatting | bytes 2097152 | tf_op jit(solution)/shard_map/convert_element_type | solution.py:37
  59.4 3.5 %all-to-all-start.1 = ((bf16[8,512,128]{2,0,1:T(8,128)(2,1)}), bf16[8,512,128]{2,0,1:T(8,128)(2,1)S(1)}, u32[]{:S(2)}, u32[]{:S(2)}) async-start(bf16[8,512,128]{2,0,1:T(8,128)(2,1)} %copy.26), calls=%async_computation.1 | async-start | bytes 2097152 | tf_op jit(solution)/shard_map/all_to_all | solution.py:83
  63.0 13.1 %all-to-all-done.1 = bf16[8,512,128]{2,0,1:T(8,128)(2,1)S(1)} async-done(((bf16[8,512,128]{2,0,1:T(8,128)(2,1)}), bf16[8,512,128]{2,0,1:T(8,128)(2,1)S(1)}, u32[]{:S(2)}, u32[]{:S(2)}) %all-to-all-start.1) | async-done | bytes 1048608 | tf_op jit(solution)/shard_map/all_to_all | solution.py:83
  76.1 0.2 copy.27
  76.4 1.7 %fusion.30 = f32[8,384,4,128]{3,1,2,0:T(8,128)S(1)} fusion(bf16[8,4,128,128]{3,2,1,0:T(8,128)(2,1)S(1)} %broadcast_multiply_fusion.1, s32[8,384]{1,0:T(8,128)S(1)} %eq.56), kind=kOutput, calls=%fused_computation.37 | convolution fusion | flops 403046400 | bytes 7352320 | tf_op jit(solution)/shard_map/kfsn,ken->fske/dot_general | solution.py:89
  78.2 3.9 %collective-permute-start.1 = (bf16[2,4,128,128]{3,2,1,0:T(8,128)(2,1)S(1)}, bf16[2,4,128,128]{3,2,1,0:T(8,128)(2,1)S(1)}, u32[]{:S(2)}, u32[]{:S(2)}) collective-permute-start(bf16[2,4,128,128]{3,2,1,0:T(8,128)(2,1)S(1)} %slice.46), channel_id=1, source_target_pairs={{0,4},{4,8},{8,12},{12,16},{16,20},{20,24},{24,28},{1,5},{5,9},{9,... | collective-permute-start | bytes 786440 | tf_op jit(solution)/shard_map/ppermute | solution.py:14
  82.2 3.2 %collective-permute-done.1 = bf16[2,4,128,128]{3,2,1,0:T(8,128)(2,1)S(1)} collective-permute-done((bf16[2,4,128,128]{3,2,1,0:T(8,128)(2,1)S(1)}, bf16[2,4,128,128]{3,2,1,0:T(8,128)(2,1)S(1)}, u32[]{:S(2)}, u32[]{:S(2)}) %collective-permute-start.1) | collective-permute-done | bytes 262176 | tf_op jit(solution)/shard_map/ppermute | solution.py:14
  85.5 4.8 %fusion.1 = f32[128,8,384]{0,2,1:T(8,128)S(1)} fusion(f32[8,384,4,128]{3,1,2,0:T(8,128)S(1)} %fusion.30, f32[4,8,384]{2,0,1:T(4,128)S(1)} %get-tuple-element.11, f32[4,8,384]{2,0,1:T(4,128)S(1)} %get-tuple-element.10, bf16[1,8,4,128,128]{4,3,0,2,1:T(8,128)(2,1)S(1)} %broadcast_multiply_fusion, bf16[1,8,4,128,128]{4,3,0,2,1:T(8,128)(2,1)S(1)} %get-tuple-element.9, ...), kind=kOutput, calls=%fused_computation.2 | convolution fusion | flops 1224474624 | bytes 11122176 | tf_op jit(solution)/shard_map/jkfsn,kejn->fske/dot_general | solution.py:93
  90.3 1.6 %copy.29 = f32[128,3072]{1,0:T(8,128)} copy(f32[128,3072]{0,1:T(8,128)S(1)} %bitcast.74) | data formatting | bytes 3145728 | tf_op jit(solution)/shard_map/reshape | solution.py:97
  (25 shorter events, 0.7 us)
Async XLA Ops:
  0.0 52.5 %copy-start = (f32[8,128,128]{2,1,0:T(8,128)S(1)}, f32[8,128,128]{2,1,0:T(8,128)}, u32[]{:S(2)}) copy-start(f32[8,128,128]{2,1,0:T(8,128)} %param.18) | copy-start | bytes 1572868
  3.8 1.9 %copy-start.2 = (s32[3072]{0:T(1024)S(1)}, s32[3072]{0:T(1024)}, u32[]{:S(2)}) copy-start(s32[3072]{0:T(1024)} %param.17) | copy-start | bytes 36868
  18.3 4.0 %copy-start.3 = (s32[3072]{0:T(1024)S(1)}, s32[3072]{0:T(1024)}, u32[]{:S(2)}) copy-start(s32[3072]{0:T(1024)} %param.16) | copy-start | bytes 36868
  18.3 14.6 %collective-permute-start = (f32[2,4,128,128]{3,2,1,0:T(8,128)S(1)}, f32[2,4,128,128]{3,2,1,0:T(8,128)S(1)}, u32[]{:S(2)}, u32[]{:S(2)}) collective-permute-start(f32[2,4,128,128]{3,2,1,0:T(8,128)S(1)} %pad_add_fusion.1), channel_id=1, source_target_pairs={{4,0},{8,4},{12,8},{16,12},{20,16},{24,20},{28,24},{5,1},{9,5},{13... | collective-permute-start | bytes 1572872 | tf_op jit(solution)/shard_map/ppermute | solution.py:14
  32.2 0.7 copy-start.4
  52.5 1.0 %copy-start.1 = (f32[8,128,128]{2,1,0:T(8,128)S(1)}, f32[8,128,128]{2,1,0:T(8,128)}, u32[]{:S(2)}) copy-start(f32[8,128,128]{2,1,0:T(8,128)} %param.19) | copy-start | bytes 1572868
  59.4 16.6 %all-to-all-start.1 = ((bf16[8,512,128]{2,0,1:T(8,128)(2,1)}), bf16[8,512,128]{2,0,1:T(8,128)(2,1)S(1)}, u32[]{:S(2)}, u32[]{:S(2)}) async-start(bf16[8,512,128]{2,0,1:T(8,128)(2,1)} %copy.26), calls=%async_computation.1 | async-start | bytes 2097152 | tf_op jit(solution)/shard_map/all_to_all | solution.py:83
  78.2 7.2 %collective-permute-start.1 = (bf16[2,4,128,128]{3,2,1,0:T(8,128)(2,1)S(1)}, bf16[2,4,128,128]{3,2,1,0:T(8,128)(2,1)S(1)}, u32[]{:S(2)}, u32[]{:S(2)}) collective-permute-start(bf16[2,4,128,128]{3,2,1,0:T(8,128)(2,1)S(1)} %slice.46), channel_id=1, source_target_pairs={{0,4},{4,8},{8,12},{12,16},{16,20},{20,24},{24,28},{1,5},{5,9},{9,... | collective-permute-start | bytes 786440 | tf_op jit(solution)/shard_map/ppermute | solution.py:14
where the time goes:
time: 92.4 us; the launch traced here: 91.9 us
  matrix products  33.3 us (36%)
  blocking collectives  19 us (21%)
  waiting for transfers between devices  16.3 us (18%)
  starting transfers between devices  9.33 us (10%)
  local copies, waits for them, and re-layouts  7.08 us (8%)
  other arithmetic  6.64 us (7%)
    all_to_all x1, blocking collectives, shards(): lax.all_to_all(restricted, 'src', split_axis=0, concat_axis=1, tiled=True)  19 us
    all_to_all x1, waiting for transfers between devices, shards(): lax.all_to_all(solved, 'src', split_axis=1, concat_axis=0, tiled=True)  13.1 us
    dot_general x1, matrix products, shards(): jnp.einsum('fske,ken->kfsn', coef_head[:, None] * resid_blocks[None], hea...  11.7 us
    dot_general x1, matrix products, shards(): jnp.einsum('fske,ken->kfsn', coef_tail[:, None] * resid_blocks[None], tai...  9.91 us
    ppermute x2, starting transfers between devices, shifted(): return lax.ppermute(x, axis, pairs)  5.81 us
    dot_general x1, matrix products, shards(): jnp.einsum('jkfsn,kejn->fske', windows, head_low, preferred_element_type=...  4.77 us
    all_to_all x1, starting transfers between devices, shards(): lax.all_to_all(solved, 'src', split_axis=1, concat_axis=0, tiled=True)  3.52 us
    ppermute x2, waiting for transfers between devices, shifted(): return lax.ppermute(x, axis, pairs)  3.22 us
  transfers between devices with their start and end apart: 3, of which 2 were waited for; matrix products, arithmetic and copies ran while one was open for 13% of the time, Pallas kernels for 0%

commit v1 on v0

--- a/solution.py
+++ b/solution.py
@@ -78,7 +78,10 @@
     keep_mask = interior.reshape(nblocks, 1, 1, bnodes)
     restricted = (nodal_sum * keep_mask.astype(jnp.float32)).astype(jnp.bfloat16)
     restricted = restricted.reshape(nblocks * 4, src_dev, bnodes)
-    grouped = lax.all_to_all(restricted, "src", split_axis=0, concat_axis=1, tiled=True)
+    grouped = jnp.concatenate(
+        lax.all_to_all(jnp.stack(jnp.split(restricted, lax.axis_size("src"), axis=0)), "src", 0, 0),
+        axis=1,
+    )
     solved = block_sweep(grouped, block_inv, block_op)
     nodal = lax.all_to_all(solved, "src", split_axis=1, concat_axis=0, tiled=True)
     nodal = nodal.reshape(nblocks, 4, src_dev, bnodes) * keep_mask.astype(jnp.bfloat16)

time: 92.4 us -> 92.4 us (level)
  no operation moved by 1% of the time
where the time goes in v1:
time: 92.4 us; the launch traced here: 91.9 us
  matrix products  33.3 us (36%)
  blocking collectives  19 us (21%)
  waiting for transfers between devices  16.3 us (18%)
  starting transfers between devices  9.33 us (10%)
  local copies, waits for them, and re-layouts  7.15 us (8%)
  other arithmetic  6.56 us (7%)
    all_to_all x1, blocking collectives, shards(): lax.all_to_all(jnp.stack(jnp.split(restricted, lax.axis_size('src'), axis...  19 us
    all_to_all x1, waiting for transfers between devices, shards(): lax.all_to_all(solved, 'src', split_axis=1, concat_axis=0, tiled=True)  13.1 us
    dot_general x1, matrix products, shards(): jnp.einsum('fske,ken->kfsn', coef_head[:, None] * resid_blocks[None], hea...  11.7 us
    dot_general x1, matrix products, shards(): jnp.einsum('fske,ken->kfsn', coef_tail[:, None] * resid_blocks[None], tai...  9.9 us
    ppermute x2, starting transfers between devices, shifted(): return lax.ppermute(x, axis, pairs)  5.81 us
    dot_general x1, matrix products, shards(): jnp.einsum('jkfsn,kejn->fske', windows, head_low, preferred_element_type=...  4.77 us
    all_to_all x1, starting transfers between devices, shards(): lax.all_to_all(solved, 'src', split_axis=1, concat_axis=0, tiled=True)  3.52 us
    ppermute x2, waiting for transfers between devices, shifted(): return lax.ppermute(x, axis, pairs)  3.22 us
  transfers between devices with their start and end apart: 3, of which 2 were waited for; matrix products, arithmetic and copies ran while one was open for 13% of the time, Pallas kernels for 0%

profile of v1, /device:TPU:1, one launch (start us, length us, event | category | flops | bytes accessed | tf_op | source)
XLA Modules:
  0.0 91.9 jit_solution(1721062712600898315)
XLA Ops:
  0.0 0.9 broadcast_multiply_fusion.2
  0.9 2.9 %multiply_subtract_fusion = f32[128,3072]{1,0:T(8,128)} fusion(f32[128,3072]{1,0:T(8,128)} %param.10, f32[3072]{0:T(1024)} %param.11, f32[128]{0:T(128)} %param.13, s32[3072]{0:T(1024)S(1)} %iota_add_fusion, s32[128]{0:T(128)} %param.12), kind=kLoop, calls=%fused_computation.33 | loop fusion | flops 1572864 | bytes 3171328 | tf_op jit(solution)/shard_map/sub | solution.py:59
  3.8 1.9 %copy.36 = f32[128,3072]{0,1:T(8,128)S(1)} copy(f32[128,3072]{1,0:T(8,128)} %multiply_subtract_fusion) | data formatting | bytes 3145728 | tf_op jit(solution)/shard_map/mul | solution.py:72
  5.7 11.7 %fusion.4 = f32[8,4,128,384]{3,2,1,0:T(8,128)S(1)} fusion(f32[128,8,384]{0,2,1:T(8,128)S(1)} %bitcast.63, f32[4,8,384]{2,0,1:T(4,128)S(1)} %get-tuple-element.15, s32[8,384]{1,0:T(8,128)S(1)} %eq.63), kind=kOutput, calls=%fused_computation.6 | convolution fusion | flops 7250509824 | bytes 7925760 | tf_op jit(solution)/shard_map/fske,ken->kfsn/dot_general | solution.py:71
  17.4 0.9 fusion.45
  18.3 1.9 %collective-permute-start = (f32[2,4,128,128]{3,2,1,0:T(8,128)S(1)}, f32[2,4,128,128]{3,2,1,0:T(8,128)S(1)}, u32[]{:S(2)}, u32[]{:S(2)}) collective-permute-start(f32[2,4,128,128]{3,2,1,0:T(8,128)S(1)} %pad_add_fusion.1), channel_id=1, source_target_pairs={{4,0},{8,4},{12,8},{16,12},{20,16},{24,20},{28,24},{5,1},{9,5},{13... | collective-permute-start | bytes 1572872 | tf_op jit(solution)/shard_map/ppermute | solution.py:14
  20.3 2.0 %pad_add_fusion = f32[10,4,128,128]{3,2,1,0:T(8,128)} fusion(f32[8,4,128,128]{3,2,1,0:T(8,128)S(1)} %get-tuple-element.6, f32[8,4,128,128]{3,2,1,0:T(8,128)S(1)} %get-tuple-element.7, f32[8,4,128,128]{3,2,1,0:T(8,128)S(1)} %get-tuple-element.5), kind=kLoop, calls=%fused_computation.22 | loop fusion | flops 1310720 | bytes 8912896 | tf_op jit(solution)/shard_map/add | solution.py:22
  22.3 9.9 %slice_add_fusion = f32[8,4,128,128]{3,2,1,0:T(8,128)S(1)} fusion(f32[10,4,128,128]{3,2,1,0:T(8,128)} %pad_add_fusion, f32[128,8,384]{0,2,1:T(8,128)S(1)} %bitcast.64, f32[4,8,384]{2,0,1:T(4,128)S(1)} %get-tuple-element.14, s32[8,384]{1,0:T(8,128)S(1)} %eq.56), kind=kOutput, calls=%fused_computation.26 | convolution fusion | flops 2418409472 | bytes 5828608 | tf_op jit(solution)/shard_map/fske,ken->kfsn/dot_general | solution.py:68
  32.3 0.6 copy-done.4
  33.0 0.3 fusion.23
  33.5 19.0 %all_to_all.20 = bf16[4,8,128,128]{3,2,1,0:T(8,128)(2,1)S(1)} all-to-all(bf16[4,8,128,128]{3,2,1,0:T(8,128)(2,1)S(1)} %pad_maximum_fusion.1), channel_id=1, replica_groups=mesh['mesh'=8,'src'=4] {'src'}, dimensions={0} | all-to-all | bytes 2097152 | tf_op jit(solution)/shard_map/all_to_all | solution.py:82
  52.5 1.0 %fusion.48 = f32[8,512,128]{2,1,0:T(8,128)S(1)} fusion(bf16[8,512,128]{2,1,0:T(8,128)(2,1)S(1)} %bitcast.67, f32[8,128,128]{2,1,0:T(8,128)S(1)} %copy-done), kind=kOutput, calls=%fused_computation.59 | convolution fusion | flops 805306368 | bytes 3670016 | tf_op jit(solution)/shard_map/ism,inm->isn/dot_general | solution.py:34
  53.6 2.0 %fusion.49 = f32[8,512,128]{2,1,0:T(8,128)S(1)} fusion(f32[8,512,128]{2,1,0:T(8,128)S(1)} %fusion.48, f32[8,128,128]{2,1,0:T(8,128)S(1)} %copy-done.1), kind=kOutput, calls=%fused_computation.60 | convolution fusion | flops 805306368 | bytes 4718592 | tf_op jit(solution)/shard_map/ism,inm->isn/dot_general | solution.py:35
  55.5 2.2 %add_convert_fusion = bf16[8,512,128]{2,1,0:T(8,128)(2,1)S(1)} fusion(f32[8,512,128]{2,1,0:T(8,128)S(1)} %fusion.48, f32[8,128,128]{2,1,0:T(8,128)S(1)} %copy-done, f32[8,512,128]{2,1,0:T(8,128)S(1)} %fusion.49, bf16[8,512,128]{2,1,0:T(8,128)(2,1)S(1)} %bitcast.68), kind=kOutput, calls=%fused_computation.29 | convolution fusion | flops 807403520 | bytes 6815744 | tf_op jit(solution)/shard_map/ism,inm->isn/dot_general | solution.py:36
  57.8 1.6 %copy.26 = bf16[8,512,128]{2,0,1:T(8,128)(2,1)} copy(bf16[8,512,128]{2,1,0:T(8,128)(2,1)S(1)} %add_convert_fusion) | data formatting | bytes 2097152 | tf_op jit(solution)/shard_map/convert_element_type | solution.py:37
  59.4 3.5 %all-to-all-start.1 = ((bf16[8,512,128]{2,0,1:T(8,128)(2,1)}), bf16[8,512,128]{2,0,1:T(8,128)(2,1)S(1)}, u32[]{:S(2)}, u32[]{:S(2)}) async-start(bf16[8,512,128]{2,0,1:T(8,128)(2,1)} %copy.26), calls=%async_computation.1 | async-start | bytes 2097152 | tf_op jit(solution)/shard_map/all_to_all | solution.py:86
  63.0 13.1 %all-to-all-done.1 = bf16[8,512,128]{2,0,1:T(8,128)(2,1)S(1)} async-done(((bf16[8,512,128]{2,0,1:T(8,128)(2,1)}), bf16[8,512,128]{2,0,1:T(8,128)(2,1)S(1)}, u32[]{:S(2)}, u32[]{:S(2)}) %all-to-all-start.1) | async-done | bytes 1048608 | tf_op jit(solution)/shard_map/all_to_all | solution.py:86
  76.1 0.2 copy.27
  76.4 1.7 %fusion.30 = f32[8,384,4,128]{3,1,2,0:T(8,128)S(1)} fusion(bf16[8,4,128,128]{3,2,1,0:T(8,128)(2,1)S(1)} %broadcast_multiply_fusion.1, s32[8,384]{1,0:T(8,128)S(1)} %eq.56), kind=kOutput, calls=%fused_computation.36 | convolution fusion | flops 403046400 | bytes 7352320 | tf_op jit(solution)/shard_map/kfsn,ken->fske/dot_general | solution.py:92
  78.2 3.9 %collective-permute-start.1 = (bf16[2,4,128,128]{3,2,1,0:T(8,128)(2,1)S(1)}, bf16[2,4,128,128]{3,2,1,0:T(8,128)(2,1)S(1)}, u32[]{:S(2)}, u32[]{:S(2)}) collective-permute-start(bf16[2,4,128,128]{3,2,1,0:T(8,128)(2,1)S(1)} %slice.50), channel_id=1, source_target_pairs={{0,4},{4,8},{8,12},{12,16},{16,20},{20,24},{24,28},{1,5},{5,9},{9,... | collective-permute-start | bytes 786440 | tf_op jit(solution)/shard_map/ppermute | solution.py:14
  82.2 3.2 %collective-permute-done.1 = bf16[2,4,128,128]{3,2,1,0:T(8,128)(2,1)S(1)} collective-permute-done((bf16[2,4,128,128]{3,2,1,0:T(8,128)(2,1)S(1)}, bf16[2,4,128,128]{3,2,1,0:T(8,128)(2,1)S(1)}, u32[]{:S(2)}, u32[]{:S(2)}) %collective-permute-start.1) | collective-permute-done | bytes 262176 | tf_op jit(solution)/shard_map/ppermute | solution.py:14
  85.4 0.1 fusion.40
  85.5 4.8 %fusion.1 = f32[128,8,384]{0,2,1:T(8,128)S(1)} fusion(f32[8,384,4,128]{3,1,2,0:T(8,128)S(1)} %fusion.30, f32[4,8,384]{2,0,1:T(4,128)S(1)} %get-tuple-element.15, f32[4,8,384]{2,0,1:T(4,128)S(1)} %get-tuple-element.14, bf16[1,8,4,128,128]{4,3,0,2,1:T(8,128)(2,1)S(1)} %broadcast_multiply_fusion, bf16[1,8,4,128,128]{4,3,0,2,1:T(8,128)(2,1)S(1)} %get-tuple-element.9, ...), kind=kOutput, calls=%fused_computation.2 | convolution fusion | flops 1224474624 | bytes 11122176 | tf_op jit(solution)/shard_map/jkfsn,kejn->fske/dot_general | solution.py:96
  90.3 1.6 %copy.29 = f32[128,3072]{1,0:T(8,128)} copy(f32[128,3072]{0,1:T(8,128)S(1)} %bitcast.71) | data formatting | bytes 3145728 | tf_op jit(solution)/shard_map/reshape | solution.py:100
  (25 shorter events, 0.7 us)
Async XLA Ops:
  0.0 52.5 %copy-start = (f32[8,128,128]{2,1,0:T(8,128)S(1)}, f32[8,128,128]{2,1,0:T(8,128)}, u32[]{:S(2)}) copy-start(f32[8,128,128]{2,1,0:T(8,128)} %param.18) | copy-start | bytes 1572868
  3.8 1.9 %copy-start.2 = (s32[3072]{0:T(1024)S(1)}, s32[3072]{0:T(1024)}, u32[]{:S(2)}) copy-start(s32[3072]{0:T(1024)} %param.17) | copy-start | bytes 36868
  18.3 4.0 %copy-start.3 = (s32[3072]{0:T(1024)S(1)}, s32[3072]{0:T(1024)}, u32[]{:S(2)}) copy-start(s32[3072]{0:T(1024)} %param.16) | copy-start | bytes 36868
  18.3 14.6 %collective-permute-start = (f32[2,4,128,128]{3,2,1,0:T(8,128)S(1)}, f32[2,4,128,128]{3,2,1,0:T(8,128)S(1)}, u32[]{:S(2)}, u32[]{:S(2)}) collective-permute-start(f32[2,4,128,128]{3,2,1,0:T(8,128)S(1)} %pad_add_fusion.1), channel_id=1, source_target_pairs={{4,0},{8,4},{12,8},{16,12},{20,16},{24,20},{28,24},{5,1},{9,5},{13... | collective-permute-start | bytes 1572872 | tf_op jit(solution)/shard_map/ppermute | solution.py:14
  32.2 0.7 copy-start.4
  52.5 1.0 %copy-start.1 = (f32[8,128,128]{2,1,0:T(8,128)S(1)}, f32[8,128,128]{2,1,0:T(8,128)}, u32[]{:S(2)}) copy-start(f32[8,128,128]{2,1,0:T(8,128)} %param.19) | copy-start | bytes 1572868
  59.4 16.7 %all-to-all-start.1 = ((bf16[8,512,128]{2,0,1:T(8,128)(2,1)}), bf16[8,512,128]{2,0,1:T(8,128)(2,1)S(1)}, u32[]{:S(2)}, u32[]{:S(2)}) async-start(bf16[8,512,128]{2,0,1:T(8,128)(2,1)} %copy.26), calls=%async_computation.1 | async-start | bytes 2097152 | tf_op jit(solution)/shard_map/all_to_all | solution.py:86
  78.2 7.2 %collective-permute-start.1 = (bf16[2,4,128,128]{3,2,1,0:T(8,128)(2,1)S(1)}, bf16[2,4,128,128]{3,2,1,0:T(8,128)(2,1)S(1)}, u32[]{:S(2)}, u32[]{:S(2)}) collective-permute-start(bf16[2,4,128,128]{3,2,1,0:T(8,128)(2,1)S(1)} %slice.50), channel_id=1, source_target_pairs={{0,4},{4,8},{8,12},{12,16},{16,20},{20,24},{24,28},{1,5},{5,9},{9,... | collective-permute-start | bytes 786440 | tf_op jit(solution)/shard_map/ppermute | solution.py:14
